TPU v7x, 1024 devices: a whole 4x8x16 slice. The times are simulated.
1024 devices in a mesh: section: 16 (over y, core), row: 16 (over z), col: 4 (over x).
Axes of the slice: x: 4, y: 8, z: 16, core: 2. Of those that a mesh axis runs over, the one named last changes fastest.
Arguments:
- inputs: bfloat16 [16, 3072, 5120], P('section', 'row', 'col'), may hold values from -12 to 12
- down_weight: bfloat16 [16, 512, 5120], P('section', 'row', 'col'), may hold values from -5 to 5
- up_weight: bfloat16 [16, 512, 8192], P('section', 'row', 'col'), may hold values from -0.25 to 0.25
- value_grad: bfloat16 [16, 3072, 8192], P('section', 'row', 'col'), may hold values from -1.1953125 to 1.1953125
Outputs:
- passed_grad: bfloat16 [16, 3072, 5120], P('section', 'row', 'col')
- down_grad: bfloat16 [16, 512, 5120], P('section', 'row', 'col')
- up_grad: bfloat16 [16, 512, 8192], P('section', 'row', 'col')
All inputs are finite; a program needn't handle non-finite values.
Results may differ from a plain program's by a relative error of at most 0.03.
Values may be sent and summed in bfloat16 or wider, within the bound.
A program may use at most 32 MiB of HBM per device.

v0:
```python
import jax
import jax.numpy as jnp
from jax import lax
from jax.sharding import PartitionSpec as P


def shifted(value, axis, steps):
    count = lax.axis_size(axis)
    leading, last = (max(0, -steps), min(count, count - steps))
    return lax.ppermute(value, axis, [(source, source + steps) for source in range(leading, last)])


def body(inputs, down_weight, up_weight, value_grad):
    tokens = inputs[0]
    cotangent = value_grad[0]
    down_full, up_full = (
        lax.all_gather(down_weight[0], "row", axis=0, tiled=True),
        lax.all_gather(up_weight[0], "row", axis=0, tiled=True),
    )
    latent_part = jnp.einsum("td,ld->tl", tokens, down_full, preferred_element_type=jnp.float32)
    grad_part = jnp.einsum("tf,lf->tl", cotangent, up_full, preferred_element_type=jnp.float32)
    latent, normed_grad = (
        lax.psum(latent_part.astype(jnp.bfloat16), "col").astype(jnp.float32),
        lax.psum(grad_part.astype(jnp.bfloat16), "col").astype(jnp.float32),
    )
    inv_rms = lax.rsqrt(jnp.mean(latent * latent, axis=-1, keepdims=True) + 1e-06)
    normed = latent * inv_rms
    normed_bf = normed.astype(jnp.bfloat16)
    inner = jnp.mean(normed_grad * normed, axis=-1, keepdims=True)
    latent_bf = (inv_rms * (normed_grad - normed * inner)).astype(jnp.bfloat16)
    picked = normed_bf
    up_grad = lax.psum_scatter(
        jnp.einsum("tl,tf->lf", picked, cotangent, preferred_element_type=jnp.float32).astype(
            jnp.bfloat16
        ),
        "row",
        scatter_dimension=0,
        tiled=True,
    )
    picked = latent_bf
    down_grad = lax.psum_scatter(
        jnp.einsum("tl,td->ld", picked, tokens, preferred_element_type=jnp.float32).astype(
            jnp.bfloat16
        ),
        "row",
        scatter_dimension=0,
        tiled=True,
    )
    input_grad = jnp.einsum(
        "tl,ld->td", latent_bf, down_full, preferred_element_type=jnp.float32
    ).astype(jnp.bfloat16)
    passed = shifted(input_grad, "section", -1)
    return (passed[None], down_grad[None], up_grad[None])


def solution(mesh):
    return jax.shard_map(
        body,
        mesh=mesh,
        in_specs=(
            P("section", "row", "col"),
            P("section", "row", "col"),
            P("section", "row", "col"),
            P("section", "row", "col"),
        ),
        out_specs=(
            P("section", "row", "col"),
            P("section", "row", "col"),
            P("section", "row", "col"),
        ),
        check_vma=False,
    )
```

profile of v0, /device:TPU:2, one launch (start us, length us, event | category | flops | bytes accessed | tf_op | source)
XLA Modules:
  0.0 400.5 jit_solution(17130589871610015330)
XLA Ops:
  7.2 0.0 all-gather.5.cloned.1.call-start
  7.2 0.7 all-gather.5.cloned.1.call-update
  7.9 0.0 all-gather.7.cloned.1.call-start
  8.0 0.7 all-gather.7.cloned.1.call-update
  8.7 0.0 all-reduce.3.cloned.1.call-start
  8.7 85.2 %all-gather.5.cloned.1.call-done = bf16[1,512,1280]{2,1,0:T(8,128)(2,1)} async-done(((bf16[1,32,1280]{2,1,0:T(8,128)(2,1)}), bf16[1,512,1280]{2,1,0:T(8,128)(2,1)}) %all-gather.5.cloned.1.call-update) | async-done | bytes 1310736 | tf_op jit(solution)/shard_map/all_gather | solution.py:17
  93.9 2.7 fusion.5
  96.7 73.4 %all-gather.7.cloned.1.call-done = bf16[1,512,2048]{2,1,0:T(8,128)(2,1)} async-done(((bf16[1,32,2048]{2,1,0:T(8,128)(2,1)}), bf16[1,512,2048]{2,1,0:T(8,128)(2,1)}) %all-gather.7.cloned.1.call-update) | async-done | bytes 2097168 | tf_op jit(solution)/shard_map/all_gather | solution.py:18
  170.0 3.1 fusion.8
  173.1 0.0 all-reduce.3.cloned.1.call-update
  173.2 0.0 reduce-scatter.3.cloned.1.call-start
  173.2 60.6 %all-reduce.3.cloned.1.call-done = (bf16[192,512]{1,0:T(8,128)(2,1)}, bf16[192,512]{1,0:T(8,128)(2,1)}) async-done(((bf16[192,512]{1,0:T(8,128)(2,1)}, bf16[192,512]{1,0:T(8,128)(2,1)}), (bf16[192,512]{1,0:T(8,128)(2,1)}, bf16[192,512]{1,0:T(8,128)(2,1)})) %all-reduce.3.cloned.1.call-update) | async-done | bytes 393232 | tf_op jit(solution)/shard_map/psum | solution.py:23
  233.8 1.0 fusion.17
  234.9 1.2 fusion.18
  236.1 2.8 convolution_convert_fusion.1
  239.0 0.0 reduce-scatter.5.cloned.1.call-start
  239.0 2.2 convolution_convert_fusion
  241.2 1.3 copy-done.1
  242.5 0.5 convolution_convert_fusion.2
  243.0 1.3 collective-permute-start
  244.3 2.5 collective-permute-done
  246.8 67.8 %reduce-scatter.3.cloned.1.call-done = bf16[32,1280]{1,0:T(8,128)(2,1)} async-done(((bf16[512,1280]{1,0:T(8,128)(2,1)}), bf16[32,1280]{1,0:T(8,128)(2,1)}) %reduce-scatter.3.cloned.1.call-update) | async-done | bytes 81936 | tf_op jit(solution)/shard_map/reduce_scatter | solution.py:41
  314.6 78.6 %reduce-scatter.5.cloned.1.call-done = bf16[32,2048]{1,0:T(8,128)(2,1)} async-done(((bf16[512,2048]{1,0:T(8,128)(2,1)}), bf16[32,2048]{1,0:T(8,128)(2,1)}) %reduce-scatter.5.cloned.1.call-update) | async-done | bytes 131088 | tf_op jit(solution)/shard_map/reduce_scatter | solution.py:32
  393.2 0.8 copy.10
  (13 shorter events, 0.1 us)
Async XLA Ops:
  7.2 162.9 %copy-start = (bf16[1,192,2048]{2,1,0:T(8,128)(2,1)S(1)}, bf16[1,192,2048]{2,1,0:T(8,128)(2,1)}, u32[]{:S(2)}) copy-start(bf16[1,192,2048]{2,1,0:T(8,128)(2,1)} %param.7) | copy-start | bytes 2359300
  7.2 86.7 %all-gather.5.cloned.1.call-start = ((), (), s32[]{:S(2)}) async-start(), calls=%async_computation.4 | async-start | bytes 1392640 | tf_op jit(solution)/shard_map/all_gather | solution.py:17
  7.9 162.1 %all-gather.7.cloned.1.call-start = ((), (), s32[]{:S(2)}) async-start(), calls=%async_computation.5 | async-start | bytes 2228224 | tf_op jit(solution)/shard_map/all_gather | solution.py:18
  8.7 225.1 %all-reduce.3.cloned.1.call-start = ((), (), s32[]{:S(2)}) async-start(), calls=%async_computation.6 | async-start | bytes 786432 | tf_op jit(solution)/shard_map/psum | solution.py:23
  96.7 139.5 %copy-start.3 = (bf16[1,192,1280]{2,1,0:T(8,128)(2,1)S(1)}, bf16[1,192,1280]{2,1,0:T(8,128)(2,1)}, u32[]{:S(2)}) copy-start(bf16[1,192,1280]{2,1,0:T(8,128)(2,1)} %param.4) | copy-start | bytes 1474564
  173.2 141.4 %reduce-scatter.3.cloned.1.call-start = ((), (), s32[]{:S(2)}) async-start(), calls=%async_computation.2 | async-start | bytes 1392640 | tf_op jit(solution)/shard_map/reduce_scatter | solution.py:41
  236.1 2.9 copy-start.2
  239.0 154.2 %reduce-scatter.5.cloned.1.call-start = ((), (), s32[]{:S(2)}) async-start(), calls=%async_computation.3 | async-start | bytes 2228224 | tf_op jit(solution)/shard_map/reduce_scatter | solution.py:32
  241.2 1.3 copy-start.1
  241.2 1.3 copy-start.4
  243.0 3.8 collective-permute-start
Sparse Core Ops, SparseCore 0:
  10.7 83.1 all-gather.4
  96.6 73.3 all-gather.6
  173.3 60.4 all-reduce.2
  239.1 75.4 reduce-scatter.2
  318.8 74.3 reduce-scatter.4
where the time goes:
time: 401 us; the launch traced here: 400 us
  waiting for transfers between devices  369 us (92%)
  between operations  13.8 us (3%)
  matrix products  11.3 us (3%)
    all_gather x1, waiting for transfers between devices, body(): lax.all_gather(down_weight[0], 'row', axis=0, tiled=True)  85.2 us
    reduce_scatter x1, waiting for transfers between devices, body(): lax.psum_scatter(jnp.einsum('tl,tf->lf', picked, cotangent, preferred_ele...  78.6 us
    all_gather x1, waiting for transfers between devices, body(): lax.all_gather(up_weight[0], 'row', axis=0, tiled=True)  73.4 us
    reduce_scatter x1, waiting for transfers between devices, body(): lax.psum_scatter(jnp.einsum('tl,td->ld', picked, tokens, preferred_elemen...  67.8 us
    psum x1, waiting for transfers between devices, body(): lax.psum(latent_part.astype(jnp.bfloat16), 'col').astype(jnp.float32)  60.6 us
  transfers between devices with their start and end apart: 6, of which 6 were waited for; matrix products, arithmetic and copies ran while one was open for 1% of the time, Pallas kernels for 0%

commit v1 on v0

v1 whole, which is shorter than its diff:
```python
import functools

import jax
import jax.numpy as jnp
from jax import lax
from jax.experimental import pallas as pl
from jax.experimental.pallas import tpu as pltpu
from jax.sharding import PartitionSpec as P

MESH = pl.DeviceIdType.MESH
F32 = jnp.float32
BF16 = jnp.bfloat16


def remote(src, dst, send, recv, device):
    return pltpu.make_async_remote_copy(
        src_ref=src, dst_ref=dst, send_sem=send, recv_sem=recv, device_id=device, device_id_type=MESH
    )


class Stream:
    def __init__(self, names, half, block, width):
        self.__dict__.update(names)
        self.half, self.block, self.width = half, block, width


def kernel(n_sec, n_row, n_col, *refs):
    (x_hbm, dw_hbm, uw_hbm, v_hbm, passed_ref, dg_ref, ug_ref) = refs[:7]
    (xs, vs, xt, vt, wd, wu, pd, pu, qd, qu, normed, nb, lb, sd, su, rd, ru, own_d, own_u, ig, zero,
     load_sem, ag_send_d, ag_recv_d, ag_send_u, ag_recv_u, x_send_d, x_recv_d, x_send_u, x_recv_u,
     rs_send_d, rs_recv_d, rs_send_u, rs_recv_u, sec_send, sec_recv, zero_sem) = refs[7:]
    half_ring = n_row // 2
    block = dw_hbm.shape[1]
    latents = n_row * block
    sec, row, col = lax.axis_index("section"), lax.axis_index("row"), lax.axis_index("col")
    right = {"row": lax.rem(row + 1, n_row)}
    left = {"row": lax.rem(row + n_row - 1, n_row)}
    peers = [{"col": lax.rem(col + j, n_col)} for j in range(1, n_col)]
    down = {"section": lax.rem(sec + n_sec - 1, n_sec)}
    up = {"section": lax.rem(sec + 1, n_sec)}

    loads = [
        pltpu.make_async_copy(dw_hbm.at[0], wd.at[0, 0:block], load_sem.at[0]),
        pltpu.make_async_copy(uw_hbm.at[0], wu.at[0, 0:block], load_sem.at[1]),
        pltpu.make_async_copy(x_hbm.at[0], xs, load_sem.at[2]),
        pltpu.make_async_copy(v_hbm.at[0], vs, load_sem.at[3]),
    ]
    for load in loads:
        load.start()
    barrier = pltpu.get_barrier_semaphore()
    for device in [right, left, down, up] + peers:
        pl.semaphore_signal(barrier, inc=1, device_id=device, device_id_type=MESH)
    pl.semaphore_wait(barrier, 4 + len(peers))
    loads[0].wait()
    loads[1].wait()

    d = Stream(dict(w=wd, at=xt, a=xs, p=pd, q=qd, lat=lb, s=sd, r=rd, own=own_d, out=dg_ref,
                    ag_send=ag_send_d, ag_recv=ag_recv_d, x_send=x_send_d, x_recv=x_recv_d,
                    rs_send=rs_send_d, rs_recv=rs_recv_d), half_ring, block, dw_hbm.shape[2])
    u = Stream(dict(w=wu, at=vt, a=vs, p=pu, q=qu, lat=nb, s=su, r=ru, own=own_u, out=ug_ref,
                    ag_send=ag_send_u, ag_recv=ag_recv_u, x_send=x_send_u, x_recv=x_recv_u,
                    rs_send=rs_send_u, rs_recv=rs_recv_u), half_ring, block, uw_hbm.shape[2])
    lo, hi = slice(0, block), slice(block, 2 * block)

    def gather_copies(t, k):
        from_lo = t.w.at[k, lo]
        from_hi = t.w.at[k, lo if isinstance(k, int) and k == 0 else hi]
        return (
            remote(from_lo, t.w.at[k + 1, lo], t.ag_send.at[0, k], t.ag_recv.at[0, k], right),
            remote(from_hi, t.w.at[k + 1, hi], t.ag_send.at[1, k], t.ag_recv.at[1, k], left),
        )

    def gather_last(t):
        k, cut = half_ring - 1, t.width // 2
        return (
            remote(t.w.at[k, lo, 0:cut], t.w.at[0, hi, 0:cut], t.ag_send.at[0, k], t.ag_recv.at[0, k], right),
            remote(t.w.at[k, hi, cut:], t.w.at[0, hi, cut:], t.ag_send.at[1, k], t.ag_recv.at[1, k], left),
        )

    def exchange(t, k):
        for j, peer in enumerate(peers):
            remote(t.p.at[k], t.q.at[j, k], t.x_send, t.x_recv, peer).start()

    def partial_latents(t, k):
        t.p[k] = jnp.dot(t.w[k], t.at[...], preferred_element_type=F32).astype(BF16)
        exchange(t, k)

    def gather_step(t, k, last):
        arrived = gather_copies(t, k - 1)
        onward = gather_last(t) if last else gather_copies(t, k)
        for before, after in zip(arrived, onward):
            before.wait_recv()
            after.start()
        partial_latents(t, k)

    def finish_gather(t):
        for copy in gather_last(t):
            copy.wait_recv()
        partial_latents(t, 0)

    for t in (d, u):
        for copy in gather_copies(t, 0):
            copy.start()
    for t in (d, u):
        cut = t.width // 2
        t.r[0, lo, 0:cut] = jnp.zeros((block, cut), BF16)
        t.r[0, hi, cut:] = jnp.zeros((block, cut), BF16)
    zero[...] = jnp.zeros_like(zero)
    loads[2].wait()
    xt[...] = xs[...].T
    loads[3].wait()
    vt[...] = vs[...].T

    @pl.loop(1, half_ring - 1)
    def _(k):
        gather_step(d, k, False)
        gather_step(u, k, False)

    gather_step(d, half_ring - 1, True)
    gather_step(u, half_ring - 1, True)
    finish_gather(d)
    finish_gather(u)

    def exchanged(t):
        pltpu.make_async_copy(t.q, t.q, t.x_recv).wait()
        total = t.p[...].astype(F32)
        for j in range(len(peers)):
            total = total + t.q[j].astype(F32)
        return total.reshape(latents, total.shape[-1])

    latent = exchanged(d)
    inv_rms = lax.rsqrt(jnp.sum(latent * latent, axis=0, keepdims=True) * (1.0 / latents) + 1e-6)
    value = latent * inv_rms
    nb[...] = value.astype(BF16)
    normed[...] = value

    def scatter_first(t):
        cut = t.width // 2
        return (
            remote(t.s.at[0, hi, 0:cut], t.r.at[0, hi, 0:cut], t.rs_send.at[0, 0], t.rs_recv.at[0, 0], right),
            remote(t.s.at[0, hi, cut:], t.r.at[0, lo, cut:], t.rs_send.at[1, 0], t.rs_recv.at[1, 0], left),
        )

    def scatter_copies(t, j):
        pair = half_ring - j
        return (
            remote(t.s.at[pair, hi], t.r.at[j, hi], t.rs_send.at[0, j], t.rs_recv.at[0, j], right),
            remote(t.s.at[pair, lo], t.r.at[j, lo], t.rs_send.at[1, j], t.rs_recv.at[1, j], left),
        )

    def product(t, pair):
        rows = pl.ds(pl.multiple_of(pair * 2 * block, 2 * block), 2 * block)
        return jnp.dot(t.lat[rows, :], t.a[...], preferred_element_type=F32)

    def scatter_start(t):
        both = product(t, 0)
        t.s[0] = both.astype(BF16)
        for copy in scatter_first(t):
            copy.start()

    def scatter_step(t, j, first):
        t.s[half_ring - j] = product(t, half_ring - j).astype(BF16)
        arrived = scatter_first(t) if first else scatter_copies(t, j - 1)
        for part, before, after in zip((hi, lo), arrived, scatter_copies(t, j)):
            before.wait_recv()
            t.s[half_ring - j, part] = (
                t.s[half_ring - j, part].astype(F32) + t.r[j - 1, part].astype(F32)
            ).astype(BF16)
            after.start()

    def scatter_end(t):
        for copy in scatter_copies(t, half_ring - 1):
            copy.wait_recv()
        last = half_ring - 1
        t.out[0] = (
            t.s[0, lo].astype(F32) + t.r[last, lo].astype(F32) + t.r[last, hi].astype(F32)
        ).astype(BF16)

    scatter_start(u)

    normed_grad = exchanged(u)
    value = normed[...]
    inner = jnp.sum(normed_grad * value, axis=0, keepdims=True) * (1.0 / latents)
    lat_grad = inv_rms * (normed_grad - value * inner)
    lb[...] = lat_grad.astype(BF16)
    scatter_start(d)

    scatter_step(u, 1, True)
    scatter_step(d, 1, True)
    ig[...] = jnp.dot(
        lb[...].T, wd[...].reshape(latents, d.width), preferred_element_type=F32
    ).astype(BF16)
    to_section = remote(ig, passed_ref.at[0], sec_send, sec_recv, down)
    fill = pltpu.make_async_copy(zero, passed_ref.at[0], zero_sem)

    @pl.when(sec > 0)
    def _():
        to_section.start()

    @pl.when(sec == n_sec - 1)
    def _():
        fill.start()

    @pl.loop(2, half_ring)
    def _(j):
        scatter_step(u, j, False)
        scatter_step(d, j, False)

    scatter_end(u)
    scatter_end(d)

    @pl.when(sec > 0)
    def _():
        to_section.wait_send()

    @pl.when(sec < n_sec - 1)
    def _():
        to_section.wait_recv()

    @pl.when(sec == n_sec - 1)
    def _():
        fill.wait()

    for t in (d, u):
        pltpu.make_async_copy(t.q, t.q, t.x_send).wait()
        for copy in gather_copies(t, 0) + gather_last(t) + scatter_first(t):
            copy.wait_send()

        @pl.loop(1, half_ring - 1)
        def _(k):
            for copy in gather_copies(t, k):
                copy.wait_send()

        @pl.loop(1, half_ring)
        def _(j):
            for copy in scatter_copies(t, j):
                copy.wait_send()


def body(n_sec, n_row, n_col, inputs, down_weight, up_weight, value_grad):
    _, tokens, width = inputs.shape
    _, block, feat = up_weight.shape
    half = n_row // 2
    latents = n_row * block
    pair = 2 * block
    dma = pltpu.SemaphoreType.DMA
    out = lambda shape: jax.ShapeDtypeStruct(shape, BF16)
    return tuple(pl.pallas_call(
        functools.partial(kernel, n_sec, n_row, n_col),
        out_shape=(out(inputs.shape), out(down_weight.shape), out(up_weight.shape)),
        in_specs=[pl.BlockSpec(memory_space=pl.ANY)] * 4,
        out_specs=(
            pl.BlockSpec(memory_space=pl.ANY),
            pl.BlockSpec(memory_space=pltpu.VMEM),
            pl.BlockSpec(memory_space=pltpu.VMEM),
        ),
        scratch_shapes=[
            pltpu.VMEM((tokens, width), BF16),
            pltpu.VMEM((tokens, feat), BF16),
            pltpu.VMEM((width, tokens), BF16),
            pltpu.VMEM((feat, tokens), BF16),
            pltpu.VMEM((half, pair, width), BF16),
            pltpu.VMEM((half, pair, feat), BF16),
            pltpu.VMEM((half, pair, tokens), BF16),
            pltpu.VMEM((half, pair, tokens), BF16),
            pltpu.VMEM((n_col - 1, half, pair, tokens), BF16),
            pltpu.VMEM((n_col - 1, half, pair, tokens), BF16),
            pltpu.VMEM((latents, tokens), F32),
            pltpu.VMEM((latents, tokens), BF16),
            pltpu.VMEM((latents, tokens), BF16),
            pltpu.VMEM((half, pair, width), BF16),
            pltpu.VMEM((half, pair, feat), BF16),
            pltpu.VMEM((half, pair, width), BF16),
            pltpu.VMEM((half, pair, feat), BF16),
            pltpu.VMEM((block, width), F32),
            pltpu.VMEM((block, feat), F32),
            pltpu.VMEM((tokens, width), BF16),
            pltpu.VMEM((tokens, width), BF16),
            dma((4,)),
            dma((2, half)), dma((2, half)), dma((2, half)), dma((2, half)),
            dma, dma, dma, dma,
            dma((2, half)), dma((2, half)), dma((2, half)), dma((2, half)),
            dma, dma, dma,
        ],
        compiler_params=pltpu.CompilerParams(
            collective_id=0, has_side_effects=True, vmem_limit_bytes=48 * 1024 * 1024
        ),
    )(inputs, down_weight, up_weight, value_grad))


def solution(mesh):
    spec = P("section", "row", "col")
    sizes = (mesh.shape["section"], mesh.shape["row"], mesh.shape["col"])
    return jax.shard_map(
        functools.partial(body, *sizes),
        mesh=mesh,
        in_specs=(spec,) * 4,
        out_specs=(spec,) * 3,
        check_vma=False,
    )
```

time: 401 us -> 111 us (0.28)
  the two profiles are of different devices: /device:TPU:2 before, /device:TPU:24 now
where the time goes in v1:
time: 111 us; the launch traced here: 110 us
  Pallas kernels  104 us (94%)
  local copies, waits for them, and re-layouts  6.02 us (5%)
    pallas_call x1, Pallas kernels, body(): pl.pallas_call(functools.partial(kernel, n_sec, n_row, n_col), out_shape=...  104 us
    unnamed x11, local copies, waits for them, and re-layouts  6.02 us

profile of v1, /device:TPU:24, one launch (start us, length us, event | category | flops | bytes accessed | tf_op | source)
XLA Modules:
  0.0 110.2 jit_solution(14778276873105414749)
XLA Ops:
  0.6 0.0 copy-start
  0.6 1.1 %copy-done = bf16[1,192,2048]{2,1,0:T(8,128)(2,1)S(1)} copy-done((bf16[1,192,2048]{2,1,0:T(8,128)(2,1)S(1)}, bf16[1,192,2048]{2,1,0:T(8,128)(2,1)}, u32[]{:S(2)}) %copy-start) | copy-done | bytes 786456
  1.8 0.0 copy-start.1
  1.8 1.0 copy-done.1
  2.8 0.0 copy-start.2
  2.8 0.9 copy-done.2
  3.7 0.0 copy-start.3
  3.7 0.9 copy-done.3
  4.6 103.6 %shard_map.67 = (bf16[1,192,1280]{2,1,0:T(8,128)(2,1)S(1)}, bf16[1,32,1280]{2,1,0:T(8,128)(2,1)S(1)}, bf16[1,32,2048]{2,1,0:T(8,128)(2,1)S(1)}) custom-call(bf16[1,192,1280]{2,1,0:T(8,128)(2,1)S(1)} %copy-done.1, bf16[1,32,1280]{2,1,0:T(8,128)(2,1)S(1)} %copy-done.3, bf16[1,32,2048]{2,1,0:T(8,128)(2,1)S(1)} %copy-done.2, bf16[1,192,2048]{2,1,0:T(8,128)(2,1)S(1)} %copy-done), custom_call_target="tpu_custom_call" | custom-call | tf_op jit(solution)/shard_map/pallas_call | solution.py:248
  108.1 0.8 copy.10
  108.9 0.6 copy.11
  109.6 0.7 copy.12
Async XLA Ops:
  0.6 1.1 %copy-start = (bf16[1,192,2048]{2,1,0:T(8,128)(2,1)S(1)}, bf16[1,192,2048]{2,1,0:T(8,128)(2,1)}, u32[]{:S(2)}) copy-start(bf16[1,192,2048]{2,1,0:T(8,128)(2,1)} %refs_3_.1) | copy-start | bytes 2359300
  1.8 1.0 copy-start.1
  2.8 0.9 copy-start.2
  3.7 0.9 copy-start.3

commit v2 on v1

v2 whole, which is shorter than its diff:
```python
import functools

import jax
import jax.numpy as jnp
from jax import lax
from jax.experimental import pallas as pl
from jax.experimental.pallas import tpu as pltpu
from jax.sharding import PartitionSpec as P

MESH = pl.DeviceIdType.MESH
F32 = jnp.float32
BF16 = jnp.bfloat16


def remote(src, dst, send, recv, device):
    return pltpu.make_async_remote_copy(
        src_ref=src, dst_ref=dst, send_sem=send, recv_sem=recv, device_id=device, device_id_type=MESH
    )


class Stream:
    def __init__(self, **refs):
        self.__dict__.update(refs)


class Chain:
    def __init__(self, stream, index, begin, end):
        self.w, self.s, self.r = stream.w, stream.s, stream.r
        self.left_part, self.right_part = slice(begin, (begin + end) // 2), slice((begin + end) // 2, end)
        self.columns = slice(begin, end)
        self.gather_send, self.gather_recv, self.scatter_send, self.scatter_recv = (
            sem.at[index] for sem in stream.sems
        )


def kernel(n_sec, n_row, n_col, *refs):
    (x_hbm, dw_hbm, uw_hbm, v_hbm, passed_ref, dg_ref, ug_ref) = refs[:7]
    (xs, vs, xt, vt, wd, wu, pd, pu, qd, qu, normed, nb, lb, sd, su, rd, ru, ig, zero, load_sem,
     gather_send, gather_recv, scatter_send, scatter_recv, x_send, x_recv, sec_send, sec_recv, zero_sem) = refs[7:]
    half_ring = n_row // 2
    block = dw_hbm.shape[1]
    latents = n_row * block
    sec, row, col = lax.axis_index("section"), lax.axis_index("row"), lax.axis_index("col")
    right = {"row": lax.rem(row + 1, n_row)}
    left = {"row": lax.rem(row + n_row - 1, n_row)}
    peers = [{"col": lax.rem(col + j, n_col)} for j in range(1, n_col)]
    down = {"section": lax.rem(sec + n_sec - 1, n_sec)}
    up = {"section": lax.rem(sec + 1, n_sec)}

    loads = [
        pltpu.make_async_copy(dw_hbm.at[0], wd.at[0, 0:block], load_sem.at[0]),
        pltpu.make_async_copy(uw_hbm.at[0], wu.at[0, 0:block], load_sem.at[1]),
        pltpu.make_async_copy(x_hbm.at[0], xs, load_sem.at[2]),
        pltpu.make_async_copy(v_hbm.at[0], vs, load_sem.at[3]),
    ]
    for load in loads:
        load.start()
    barrier = pltpu.get_barrier_semaphore()
    for device in [right, left, down, up] + peers:
        pl.semaphore_signal(barrier, inc=1, device_id=device, device_id_type=MESH)
    pl.semaphore_wait(barrier, 4 + len(peers))
    loads[0].wait()
    loads[1].wait()

    sems = (gather_send, gather_recv, scatter_send, scatter_recv)
    d = Stream(w=wd, at=xt, a=xs, p=pd, q=qd, lat=lb, s=sd, r=rd, out=dg_ref, sems=sems,
               x_send=x_send.at[0], x_recv=x_recv.at[0])
    u = Stream(w=wu, at=vt, a=vs, p=pu, q=qu, lat=nb, s=su, r=ru, out=ug_ref, sems=sems,
               x_send=x_send.at[1], x_recv=x_recv.at[1])
    width, feat = xs.shape[1], vs.shape[1]
    d.chains = [Chain(d, 0, 0, width)]
    u.chains = [Chain(u, 1, 0, feat // 2), Chain(u, 2, feat // 2, feat)]
    chains = d.chains + u.chains
    lo, hi = slice(0, block), slice(block, 2 * block)

    def gather_copies(c, k):
        from_hi = lo if isinstance(k, int) and k == 0 else hi
        return (
            remote(c.w.at[k, lo, c.columns], c.w.at[k + 1, lo, c.columns],
                   c.gather_send.at[0, k], c.gather_recv.at[0, k], right),
            remote(c.w.at[k, from_hi, c.columns], c.w.at[k + 1, hi, c.columns],
                   c.gather_send.at[1, k], c.gather_recv.at[1, k], left),
        )

    def gather_last(c):
        k = half_ring - 1
        return (
            remote(c.w.at[k, lo, c.left_part], c.w.at[0, hi, c.left_part],
                   c.gather_send.at[0, k], c.gather_recv.at[0, k], right),
            remote(c.w.at[k, hi, c.right_part], c.w.at[0, hi, c.right_part],
                   c.gather_send.at[1, k], c.gather_recv.at[1, k], left),
        )

    def pass_on(c, k):
        last = isinstance(k, int) and k == half_ring - 1
        for before, after in zip(gather_copies(c, k - 1), gather_last(c) if last else gather_copies(c, k)):
            before.wait_recv()
            after.start()

    def arrive_last(c):
        for copy in gather_last(c):
            copy.wait_recv()

    def partial_latents(t, k):
        t.p[k] = jnp.dot(t.w[k], t.at[...], preferred_element_type=F32).astype(BF16)
        for j, peer in enumerate(peers):
            remote(t.p.at[k], t.q.at[j, k], t.x_send, t.x_recv, peer).start()

    def exchanged(t):
        pltpu.make_async_copy(t.q, t.q, t.x_recv).wait()
        total = t.p[...].astype(F32)
        for j in range(len(peers)):
            total = total + t.q[j].astype(F32)
        return total.reshape(latents, total.shape[-1])

    def scatter_first(c):
        return (
            remote(c.s.at[0, hi, c.left_part], c.r.at[0, hi, c.left_part],
                   c.scatter_send.at[0, 0], c.scatter_recv.at[0, 0], right),
            remote(c.s.at[0, hi, c.right_part], c.r.at[0, lo, c.right_part],
                   c.scatter_send.at[1, 0], c.scatter_recv.at[1, 0], left),
        )

    def scatter_copies(c, j):
        pair = half_ring - j
        return (
            remote(c.s.at[pair, hi, c.columns], c.r.at[j, hi, c.columns],
                   c.scatter_send.at[0, j], c.scatter_recv.at[0, j], right),
            remote(c.s.at[pair, lo, c.columns], c.r.at[j, lo, c.columns],
                   c.scatter_send.at[1, j], c.scatter_recv.at[1, j], left),
        )

    def product(t, pair):
        rows = slice(pair * 2 * block, (pair + 1) * 2 * block)
        t.s[pair] = jnp.dot(t.lat[rows, :], t.a[...], preferred_element_type=F32).astype(BF16)

    def scatter_start(t):
        product(t, 0)
        for c in t.chains:
            for copy in scatter_first(c):
                copy.start()

    def scatter_step(t, j):
        pair = half_ring - j
        product(t, pair)
        for c in t.chains:
            arrived = scatter_first(c) if j == 1 else scatter_copies(c, j - 1)
            for part, before, after in zip((hi, lo), arrived, scatter_copies(c, j)):
                before.wait_recv()
                t.s[pair, part, c.columns] = (
                    t.s[pair, part, c.columns].astype(F32) + t.r[j - 1, part, c.columns].astype(F32)
                ).astype(BF16)
                after.start()

    def scatter_end(t):
        last = half_ring - 1
        for c in t.chains:
            for copy in scatter_copies(c, last):
                copy.wait_recv()
        t.out[0] = (
            t.s[0, lo].astype(F32) + t.r[last, lo].astype(F32) + t.r[last, hi].astype(F32)
        ).astype(BF16)

    for c in chains:
        for copy in gather_copies(c, 0):
            copy.start()
    for c in chains:
        c.r[0, lo, c.left_part] = jnp.zeros((block, c.left_part.stop - c.left_part.start), BF16)
        c.r[0, hi, c.right_part] = jnp.zeros((block, c.right_part.stop - c.right_part.start), BF16)
    zero[...] = jnp.zeros_like(zero)
    loads[2].wait()
    xt[...] = xs[...].T
    loads[3].wait()
    vt[...] = vs[...].T

    ahead = (half_ring - 2) // 2

    @pl.loop(1, ahead + 1)
    def _(i):
        pass_on(d.chains[0], 2 * i - 1)
        partial_latents(d, 2 * i - 1)
        pass_on(u.chains[0], i)
        pass_on(d.chains[0], 2 * i)
        partial_latents(d, 2 * i)
        pass_on(u.chains[1], i)
        partial_latents(u, i)

    def up_gather(k):
        for c in u.chains:
            pass_on(c, k)
        partial_latents(u, k)

    pass_on(d.chains[0], half_ring - 1)
    partial_latents(d, half_ring - 1)
    rest = list(range(ahead + 1, half_ring))
    if len(rest) > 1:
        up_gather(rest.pop(0))
    arrive_last(d.chains[0])
    partial_latents(d, 0)
    if len(rest) > 2:
        up_gather(rest.pop(0))

    latent = exchanged(d)
    inv_rms = lax.rsqrt(jnp.sum(latent * latent, axis=0, keepdims=True) * (1.0 / latents) + 1e-6)
    value = latent * inv_rms
    nb[...] = value.astype(BF16)
    normed[...] = value

    if len(rest) > 1:
        up_gather(rest.pop(0))
    scatter_start(u)
    for k in rest:
        up_gather(k)
    scatter_step(u, 1)
    for c in u.chains:
        arrive_last(c)
    partial_latents(u, 0)
    up_steps, down_steps = list(range(2, half_ring)), list(range(1, half_ring))
    if len(up_steps) > 1:
        scatter_step(u, up_steps.pop(0))

    normed_grad = exchanged(u)
    value = normed[...]
    inner = jnp.sum(normed_grad * value, axis=0, keepdims=True) * (1.0 / latents)
    lat_grad = inv_rms * (normed_grad - value * inner)
    lb[...] = lat_grad.astype(BF16)
    scatter_start(d)
    if len(up_steps) > 1:
        scatter_step(u, up_steps.pop(0))
    scatter_step(d, down_steps.pop(0))

    ig[...] = jnp.dot(
        lb[...].T, wd[...].reshape(latents, width), preferred_element_type=F32
    ).astype(BF16)
    to_section = remote(ig, passed_ref.at[0], sec_send, sec_recv, down)
    fill = pltpu.make_async_copy(zero, passed_ref.at[0], zero_sem)

    @pl.when(sec > 0)
    def _():
        to_section.start()

    @pl.when(sec == n_sec - 1)
    def _():
        fill.start()

    while up_steps or down_steps:
        if len(down_steps) > len(up_steps) and down_steps:
            scatter_step(d, down_steps.pop(0))
        if up_steps:
            scatter_step(u, up_steps.pop(0))
        if down_steps:
            scatter_step(d, down_steps.pop(0))

    scatter_end(u)
    scatter_end(d)

    @pl.when(sec > 0)
    def _():
        to_section.wait_send()

    @pl.when(sec < n_sec - 1)
    def _():
        to_section.wait_recv()

    @pl.when(sec == n_sec - 1)
    def _():
        fill.wait()

    for t in (d, u):
        pltpu.make_async_copy(t.q, t.q, t.x_send).wait()
    for c in chains:
        for copy in gather_copies(c, 0) + gather_last(c) + scatter_first(c):
            copy.wait_send()

        @pl.loop(1, half_ring - 1)
        def _(k):
            for copy in gather_copies(c, k):
                copy.wait_send()

        @pl.loop(1, half_ring)
        def _(j):
            for copy in scatter_copies(c, j):
                copy.wait_send()


def hand_over(*refs):
    n = (len(refs) - 1) // 2
    copies = [pltpu.make_async_copy(refs[i], refs[n + i], refs[-1].at[i]) for i in range(n)]
    for copy in copies:
        copy.start()
    for copy in copies:
        copy.wait()


def body(n_sec, n_row, n_col, inputs, down_weight, up_weight, value_grad):
    _, tokens, width = inputs.shape
    _, block, feat = up_weight.shape
    half = n_row // 2
    latents = n_row * block
    pair = 2 * block
    dma = pltpu.SemaphoreType.DMA
    out = lambda shape: jax.ShapeDtypeStruct(shape, BF16)
    hbm = pl.BlockSpec(memory_space=pltpu.HBM)
    results = pl.pallas_call(
        functools.partial(kernel, n_sec, n_row, n_col),
        out_shape=(out(inputs.shape), out(down_weight.shape), out(up_weight.shape)),
        in_specs=[hbm] * 4,
        out_specs=(
            hbm,
            pl.BlockSpec(memory_space=pltpu.VMEM),
            pl.BlockSpec(memory_space=pltpu.VMEM),
        ),
        scratch_shapes=[
            pltpu.VMEM((tokens, width), BF16),
            pltpu.VMEM((tokens, feat), BF16),
            pltpu.VMEM((width, tokens), BF16),
            pltpu.VMEM((feat, tokens), BF16),
            pltpu.VMEM((half, pair, width), BF16),
            pltpu.VMEM((half, pair, feat), BF16),
            pltpu.VMEM((half, pair, tokens), BF16),
            pltpu.VMEM((half, pair, tokens), BF16),
            pltpu.VMEM((n_col - 1, half, pair, tokens), BF16),
            pltpu.VMEM((n_col - 1, half, pair, tokens), BF16),
            pltpu.VMEM((latents, tokens), F32),
            pltpu.VMEM((latents, tokens), BF16),
            pltpu.VMEM((latents, tokens), BF16),
            pltpu.VMEM((half, pair, width), BF16),
            pltpu.VMEM((half, pair, feat), BF16),
            pltpu.VMEM((half, pair, width), BF16),
            pltpu.VMEM((half, pair, feat), BF16),
            pltpu.VMEM((tokens, width), BF16),
            pltpu.VMEM((tokens, width), BF16),
            dma((4,)),
            dma((3, 2, half)), dma((3, 2, half)), dma((3, 2, half)), dma((3, 2, half)),
            dma((2,)), dma((2,)),
            dma, dma, dma,
        ],
        compiler_params=pltpu.CompilerParams(
            collective_id=0, has_side_effects=True, vmem_limit_bytes=56 * 1024 * 1024
        ),
    )(inputs, down_weight, up_weight, value_grad)
    return tuple(pl.pallas_call(
        hand_over,
        out_shape=tuple(out(r.shape) for r in results),
        in_specs=[hbm] * 3,
        out_specs=(hbm,) * 3,
        scratch_shapes=[dma((3,))],
    )(*results))


def solution(mesh):
    spec = P("section", "row", "col")
    sizes = (mesh.shape["section"], mesh.shape["row"], mesh.shape["col"])
    return jax.shard_map(
        functools.partial(body, *sizes),
        mesh=mesh,
        in_specs=(spec,) * 4,
        out_specs=(spec,) * 3,
        check_vma=False,
    )
```

time: 111 us -> 129 us (1.16)
  Pallas kernels: 104 us -> 129 us
  local copies, waits for them, and re-layouts: 6.02 us -> 0 us
    pallas_call x0 -> x1, Pallas kernels: none -> 22.5 us  [body(): pl.pallas_call(hand_over, out_shape=tuple((out(r.shape) for r in results)...]
    unnamed x11 -> x0, local copies, waits for them, and re-layouts: 6.02 us -> none
    pallas_call x1, Pallas kernels: 104 us -> 106 us  [body(): pl.pallas_call(functools.partial(kernel, n_sec, n_row, n_col), out_shape=...]
where the time goes in v2:
time: 129 us
  Pallas kernels  129 us (100%)
    pallas_call x1, Pallas kernels, body(): pl.pallas_call(functools.partial(kernel, n_sec, n_row, n_col), out_shape=...  106 us
    pallas_call x1, Pallas kernels, body(): pl.pallas_call(hand_over, out_shape=tuple((out(r.shape) for r in results)...  22.5 us

profile of v2, /device:TPU:24, one launch (start us, length us, event | category | flops | bytes accessed | tf_op | source)
XLA Modules:
  0.0 129.3 jit_solution(5536560894046267943)
XLA Ops:
  0.6 106.2 %shard_map.67 = (bf16[1,192,1280]{2,1,0:T(8,128)(2,1)}, bf16[1,32,1280]{2,1,0:T(8,128)(2,1)}, bf16[1,32,2048]{2,1,0:T(8,128)(2,1)}) custom-call(bf16[1,192,1280]{2,1,0:T(8,128)(2,1)} %refs_0_.1, bf16[1,32,1280]{2,1,0:T(8,128)(2,1)} %refs_1_.1, bf16[1,32,2048]{2,1,0:T(8,128)(2,1)} %refs_2_.1, bf16[1,192,2048]{2,1,0:T(8,128)(2,1)} %refs_3_.1), custom_call_target="tpu_custom_call" | custom-call | tf_op jit(solution)/shard_map/pallas_call | solution.py:304
  106.8 22.5 %shard_map.68 = (bf16[1,192,1280]{2,1,0:T(8,128)(2,1)}, bf16[1,32,1280]{2,1,0:T(8,128)(2,1)}, bf16[1,32,2048]{2,1,0:T(8,128)(2,1)}) custom-call(bf16[1,192,1280]{2,1,0:T(8,128)(2,1)} %get-tuple-element.6.refs_0_, bf16[1,32,1280]{2,1,0:T(8,128)(2,1)} %get-tuple-element.7.refs_1_, bf16[1,32,2048]{2,1,0:T(8,128)(2,1)} %get-tuple-element.8.refs_2_), custom_call_target="tpu_custom_call" | custom-call | tf_op jit(solution)/shard_map/pallas_call | solution.py:342

commit v3 on v2

--- a/solution.py
+++ b/solution.py
@@ -7,6 +7,9 @@
 from jax.experimental.pallas import tpu as pltpu
 from jax.sharding import PartitionSpec as P
 
+DOWN_CUTS = (0, 1)
+UP_CUTS = (0, 1, 2)
+N_CHAINS = len(DOWN_CUTS) + len(UP_CUTS) - 2
 MESH = pl.DeviceIdType.MESH
 F32 = jnp.float32
 BF16 = jnp.bfloat16
@@ -68,8 +71,10 @@
     u = Stream(w=wu, at=vt, a=vs, p=pu, q=qu, lat=nb, s=su, r=ru, out=ug_ref, sems=sems,
                x_send=x_send.at[1], x_recv=x_recv.at[1])
     width, feat = xs.shape[1], vs.shape[1]
-    d.chains = [Chain(d, 0, 0, width)]
-    u.chains = [Chain(u, 1, 0, feat // 2), Chain(u, 2, feat // 2, feat)]
+    for t, cuts in ((d, DOWN_CUTS), (u, UP_CUTS)):
+        first = 0 if t is d else len(DOWN_CUTS) - 1
+        ends = [t.w.shape[2] * cut // cuts[-1] for cut in cuts]
+        t.chains = [Chain(t, first + i, ends[i], ends[i + 1]) for i in range(len(ends) - 1)]
     chains = d.chains + u.chains
     lo, hi = slice(0, block), slice(block, 2 * block)
 
@@ -173,51 +178,28 @@
     loads[3].wait()
     vt[...] = vs[...].T
 
-    ahead = (half_ring - 2) // 2
-
-    @pl.loop(1, ahead + 1)
-    def _(i):
-        pass_on(d.chains[0], 2 * i - 1)
-        partial_latents(d, 2 * i - 1)
-        pass_on(u.chains[0], i)
-        pass_on(d.chains[0], 2 * i)
-        partial_latents(d, 2 * i)
-        pass_on(u.chains[1], i)
-        partial_latents(u, i)
-
-    def up_gather(k):
-        for c in u.chains:
-            pass_on(c, k)
-        partial_latents(u, k)
-
-    pass_on(d.chains[0], half_ring - 1)
-    partial_latents(d, half_ring - 1)
-    rest = list(range(ahead + 1, half_ring))
-    if len(rest) > 1:
-        up_gather(rest.pop(0))
-    arrive_last(d.chains[0])
-    partial_latents(d, 0)
-    if len(rest) > 2:
-        up_gather(rest.pop(0))
+    @pl.loop(1, half_ring - 1)
+    def _(k):
+        for t in (d, u):
+            for c in t.chains:
+                pass_on(c, k)
+            partial_latents(t, k)
+
+    for t in (d, u):
+        for c in t.chains:
+            pass_on(c, half_ring - 1)
+        partial_latents(t, half_ring - 1)
+    for t in (d, u):
+        for c in t.chains:
+            arrive_last(c)
+        partial_latents(t, 0)
 
     latent = exchanged(d)
     inv_rms = lax.rsqrt(jnp.sum(latent * latent, axis=0, keepdims=True) * (1.0 / latents) + 1e-6)
     value = latent * inv_rms
     nb[...] = value.astype(BF16)
     normed[...] = value
-
-    if len(rest) > 1:
-        up_gather(rest.pop(0))
     scatter_start(u)
-    for k in rest:
-        up_gather(k)
-    scatter_step(u, 1)
-    for c in u.chains:
-        arrive_last(c)
-    partial_latents(u, 0)
-    up_steps, down_steps = list(range(2, half_ring)), list(range(1, half_ring))
-    if len(up_steps) > 1:
-        scatter_step(u, up_steps.pop(0))
 
     normed_grad = exchanged(u)
     value = normed[...]
@@ -225,9 +207,9 @@
     lat_grad = inv_rms * (normed_grad - value * inner)
     lb[...] = lat_grad.astype(BF16)
     scatter_start(d)
-    if len(up_steps) > 1:
-        scatter_step(u, up_steps.pop(0))
-    scatter_step(d, down_steps.pop(0))
+
+    scatter_step(u, 1)
+    scatter_step(d, 1)
 
     ig[...] = jnp.dot(
         lb[...].T, wd[...].reshape(latents, width), preferred_element_type=F32
@@ -243,13 +225,9 @@
     def _():
         fill.start()
 
-    while up_steps or down_steps:
-        if len(down_steps) > len(up_steps) and down_steps:
-            scatter_step(d, down_steps.pop(0))
-        if up_steps:
-            scatter_step(u, up_steps.pop(0))
-        if down_steps:
-            scatter_step(d, down_steps.pop(0))
+    for j in range(2, half_ring):
+        scatter_step(u, j)
+        scatter_step(d, j)
 
     scatter_end(u)
     scatter_end(d)
@@ -284,12 +262,16 @@
 
 
 def hand_over(*refs):
-    n = (len(refs) - 1) // 2
-    copies = [pltpu.make_async_copy(refs[i], refs[n + i], refs[-1].at[i]) for i in range(n)]
-    for copy in copies:
-        copy.start()
-    for copy in copies:
-        copy.wait()
+    results, outs, held, (in_sem, out_sem) = refs[0:3], refs[3:6], refs[6:9], refs[9:]
+    reads = [pltpu.make_async_copy(results[i], held[i], in_sem.at[i]) for i in range(3)]
+    writes = [pltpu.make_async_copy(held[i], outs[i], out_sem.at[i]) for i in range(3)]
+    for read in reads:
+        read.start()
+    for read, write in zip(reads, writes):
+        read.wait()
+        write.start()
+    for write in writes:
+        write.wait()
 
 
 def body(n_sec, n_row, n_col, inputs, down_weight, up_weight, value_grad):
@@ -331,7 +313,7 @@
             pltpu.VMEM((tokens, width), BF16),
             pltpu.VMEM((tokens, width), BF16),
             dma((4,)),
-            dma((3, 2, half)), dma((3, 2, half)), dma((3, 2, half)), dma((3, 2, half)),
+            dma((N_CHAINS, 2, half)), dma((N_CHAINS, 2, half)), dma((N_CHAINS, 2, half)), dma((N_CHAINS, 2, half)),
             dma((2,)), dma((2,)),
             dma, dma, dma,
         ],
@@ -344,7 +326,7 @@
         out_shape=tuple(out(r.shape) for r in results),
         in_specs=[hbm] * 3,
         out_specs=(hbm,) * 3,
-        scratch_shapes=[dma((3,))],
+        scratch_shapes=[pltpu.VMEM(r.shape, BF16) for r in results] + [dma((3,)), dma((3,))],
     )(*results))
 
 

time: 129 us -> 102 us (0.79)
  Pallas kernels: 129 us -> 101 us
    pallas_call x1, Pallas kernels: 22.5 us -> 1.93 us  [body(): pl.pallas_call(hand_over, out_shape=tuple((out(r.shape) for r in results)...]
    pallas_call x1, Pallas kernels: 106 us -> 99.5 us  [body(): pl.pallas_call(functools.partial(kernel, n_sec, n_row, n_col), out_shape=...]
where the time goes in v3:
time: 102 us
  Pallas kernels  101 us (99%)
    pallas_call x1, Pallas kernels, body(): pl.pallas_call(functools.partial(kernel, n_sec, n_row, n_col), out_shape=...  99.5 us

profile of v3, /device:TPU:24, one launch (start us, length us, event | category | flops | bytes accessed | tf_op | source)
XLA Modules:
  0.0 102.1 jit_solution(11415727221814463436)
XLA Ops:
  0.6 99.5 %shard_map.67 = (bf16[1,192,1280]{2,1,0:T(8,128)(2,1)}, bf16[1,32,1280]{2,1,0:T(8,128)(2,1)}, bf16[1,32,2048]{2,1,0:T(8,128)(2,1)}) custom-call(bf16[1,192,1280]{2,1,0:T(8,128)(2,1)} %refs_0_.1, bf16[1,32,1280]{2,1,0:T(8,128)(2,1)} %refs_1_.1, bf16[1,32,2048]{2,1,0:T(8,128)(2,1)} %refs_2_.1, bf16[1,192,2048]{2,1,0:T(8,128)(2,1)} %refs_3_.1), custom_call_target="tpu_custom_call" | custom-call | tf_op jit(solution)/shard_map/pallas_call | solution.py:286
  100.2 1.9 %shard_map.68 = (bf16[1,192,1280]{2,1,0:T(8,128)(2,1)}, bf16[1,32,1280]{2,1,0:T(8,128)(2,1)}, bf16[1,32,2048]{2,1,0:T(8,128)(2,1)}) custom-call(bf16[1,192,1280]{2,1,0:T(8,128)(2,1)} %get-tuple-element.6.refs_0_, bf16[1,32,1280]{2,1,0:T(8,128)(2,1)} %get-tuple-element.7.refs_1_, bf16[1,32,2048]{2,1,0:T(8,128)(2,1)} %get-tuple-element.8.refs_2_), custom_call_target="tpu_custom_call" | custom-call | tf_op jit(solution)/shard_map/pallas_call | solution.py:324

commit v4 on v3

--- a/solution.py
+++ b/solution.py
@@ -38,8 +38,8 @@
 
 def kernel(n_sec, n_row, n_col, *refs):
     (x_hbm, dw_hbm, uw_hbm, v_hbm, passed_ref, dg_ref, ug_ref) = refs[:7]
-    (xs, vs, xt, vt, wd, wu, pd, pu, qd, qu, normed, nb, lb, sd, su, rd, ru, ig, zero, load_sem,
-     gather_send, gather_recv, scatter_send, scatter_recv, x_send, x_recv, sec_send, sec_recv, zero_sem) = refs[7:]
+    (xs, vs, xt, vt, wd, wu, pd, pu, qd, qu, normed, grads, nb, lb, sd, su, rd, ru, ig, load_sem,
+     gather_send, gather_recv, scatter_send, scatter_recv, x_send, x_recv, sec_send, sec_recv) = refs[7:]
     half_ring = n_row // 2
     block = dw_hbm.shape[1]
     latents = n_row * block
@@ -109,14 +109,16 @@
     def partial_latents(t, k):
         t.p[k] = jnp.dot(t.w[k], t.at[...], preferred_element_type=F32).astype(BF16)
         for j, peer in enumerate(peers):
-            remote(t.p.at[k], t.q.at[j, k], t.x_send, t.x_recv, peer).start()
-
-    def exchanged(t):
-        pltpu.make_async_copy(t.q, t.q, t.x_recv).wait()
-        total = t.p[...].astype(F32)
+            last = isinstance(k, int) and k == 0
+            remote(t.p.at[k], t.q.at[j, k], t.x_send, t.x_recv.at[1 if last else 0], peer).start()
+
+    def exchanged(t, pairs, sem):
+        arrived = t.q.at[:, pairs]
+        pltpu.make_async_copy(arrived, arrived, t.x_recv.at[sem]).wait()
+        total = t.p[pairs].astype(F32)
         for j in range(len(peers)):
-            total = total + t.q[j].astype(F32)
-        return total.reshape(latents, total.shape[-1])
+            total = total + t.q[j, pairs].astype(F32)
+        return total.reshape(-1, total.shape[-1])
 
     def scatter_first(c):
         return (
@@ -172,7 +174,6 @@
     for c in chains:
         c.r[0, lo, c.left_part] = jnp.zeros((block, c.left_part.stop - c.left_part.start), BF16)
         c.r[0, hi, c.right_part] = jnp.zeros((block, c.right_part.stop - c.right_part.start), BF16)
-    zero[...] = jnp.zeros_like(zero)
     loads[2].wait()
     xt[...] = xs[...].T
     loads[3].wait()
@@ -189,24 +190,39 @@
         for c in t.chains:
             pass_on(c, half_ring - 1)
         partial_latents(t, half_ring - 1)
-    for t in (d, u):
-        for c in t.chains:
-            arrive_last(c)
-        partial_latents(t, 0)
-
-    latent = exchanged(d)
-    inv_rms = lax.rsqrt(jnp.sum(latent * latent, axis=0, keepdims=True) * (1.0 / latents) + 1e-6)
-    value = latent * inv_rms
-    nb[...] = value.astype(BF16)
-    normed[...] = value
+    early, final = slice(1, half_ring), slice(0, 1)
+    head, rest = slice(0, 2 * block), slice(2 * block, latents)
+
+    def total_of(value):
+        return jnp.sum(value, axis=0, keepdims=True)
+
+    for c in d.chains:
+        arrive_last(c)
+    partial_latents(d, 0)
+    latent_early = exchanged(d, early, 0)
+    normed[rest, :] = latent_early
+    squares = total_of(latent_early * latent_early)
+    for c in u.chains:
+        arrive_last(c)
+    partial_latents(u, 0)
+
+    latent_final = exchanged(d, final, 1)
+    inv_rms = lax.rsqrt((squares + total_of(latent_final * latent_final)) * (1.0 / latents) + 1e-6)
+    value_final = latent_final * inv_rms
+    nb[head, :] = value_final.astype(BF16)
     scatter_start(u)
-
-    normed_grad = exchanged(u)
-    value = normed[...]
-    inner = jnp.sum(normed_grad * value, axis=0, keepdims=True) * (1.0 / latents)
-    lat_grad = inv_rms * (normed_grad - value * inner)
-    lb[...] = lat_grad.astype(BF16)
+    value = normed[rest, :] * inv_rms
+    nb[rest, :] = value.astype(BF16)
+    normed[rest, :] = value
+
+    grad_early = exchanged(u, early, 0)
+    grads[rest, :] = grad_early
+    inner = total_of(grad_early * value)
+    grad_final = exchanged(u, final, 1)
+    inner = (inner + total_of(grad_final * value_final)) * (1.0 / latents)
+    lb[head, :] = (inv_rms * (grad_final - value_final * inner)).astype(BF16)
     scatter_start(d)
+    lb[rest, :] = (inv_rms * (grads[rest, :] - normed[rest, :] * inner)).astype(BF16)
 
     scatter_step(u, 1)
     scatter_step(d, 1)
@@ -215,7 +231,6 @@
         lb[...].T, wd[...].reshape(latents, width), preferred_element_type=F32
     ).astype(BF16)
     to_section = remote(ig, passed_ref.at[0], sec_send, sec_recv, down)
-    fill = pltpu.make_async_copy(zero, passed_ref.at[0], zero_sem)
 
     @pl.when(sec > 0)
     def _():
@@ -223,7 +238,7 @@
 
     @pl.when(sec == n_sec - 1)
     def _():
-        fill.start()
+        passed_ref[...] = jnp.zeros_like(passed_ref)
 
     for j in range(2, half_ring):
         scatter_step(u, j)
@@ -239,10 +254,6 @@
     @pl.when(sec < n_sec - 1)
     def _():
         to_section.wait_recv()
-
-    @pl.when(sec == n_sec - 1)
-    def _():
-        fill.wait()
 
     for t in (d, u):
         pltpu.make_async_copy(t.q, t.q, t.x_send).wait()
@@ -262,16 +273,11 @@
 
 
 def hand_over(*refs):
-    results, outs, held, (in_sem, out_sem) = refs[0:3], refs[3:6], refs[6:9], refs[9:]
-    reads = [pltpu.make_async_copy(results[i], held[i], in_sem.at[i]) for i in range(3)]
-    writes = [pltpu.make_async_copy(held[i], outs[i], out_sem.at[i]) for i in range(3)]
-    for read in reads:
-        read.start()
-    for read, write in zip(reads, writes):
-        read.wait()
-        write.start()
-    for write in writes:
-        write.wait()
+    copies = [pltpu.make_async_copy(refs[i], refs[3 + i], refs[6].at[i]) for i in range(3)]
+    for copy in copies:
+        copy.start()
+    for copy in copies:
+        copy.wait()
 
 
 def body(n_sec, n_row, n_col, inputs, down_weight, up_weight, value_grad):
@@ -288,7 +294,7 @@
         out_shape=(out(inputs.shape), out(down_weight.shape), out(up_weight.shape)),
         in_specs=[hbm] * 4,
         out_specs=(
-            hbm,
+            pl.BlockSpec(memory_space=pltpu.VMEM),
             pl.BlockSpec(memory_space=pltpu.VMEM),
             pl.BlockSpec(memory_space=pltpu.VMEM),
         ),
@@ -304,6 +310,7 @@
             pltpu.VMEM((n_col - 1, half, pair, tokens), BF16),
             pltpu.VMEM((n_col - 1, half, pair, tokens), BF16),
             pltpu.VMEM((latents, tokens), F32),
+            pltpu.VMEM((latents, tokens), F32),
             pltpu.VMEM((latents, tokens), BF16),
             pltpu.VMEM((latents, tokens), BF16),
             pltpu.VMEM((half, pair, width), BF16),
@@ -311,23 +318,22 @@
             pltpu.VMEM((half, pair, width), BF16),
             pltpu.VMEM((half, pair, feat), BF16),
             pltpu.VMEM((tokens, width), BF16),
-            pltpu.VMEM((tokens, width), BF16),
             dma((4,)),
             dma((N_CHAINS, 2, half)), dma((N_CHAINS, 2, half)), dma((N_CHAINS, 2, half)), dma((N_CHAINS, 2, half)),
-            dma((2,)), dma((2,)),
-            dma, dma, dma,
+            dma((2,)), dma((2, 2)),
+            dma, dma,
         ],
         compiler_params=pltpu.CompilerParams(
-            collective_id=0, has_side_effects=True, vmem_limit_bytes=56 * 1024 * 1024
+            collective_id=0, has_side_effects=True, vmem_limit_bytes=40 * 1024 * 1024
         ),
-    )(inputs, down_weight, up_weight, value_grad)
+    )(*(pltpu.with_memory_space_constraint(a, pltpu.HBM) for a in (inputs, down_weight, up_weight, value_grad)))
     return tuple(pl.pallas_call(
         hand_over,
         out_shape=tuple(out(r.shape) for r in results),
-        in_specs=[hbm] * 3,
+        in_specs=[pl.BlockSpec(memory_space=pltpu.VMEM)] * 3,
         out_specs=(hbm,) * 3,
-        scratch_shapes=[pltpu.VMEM(r.shape, BF16) for r in results] + [dma((3,)), dma((3,))],
-    )(*results))
+        scratch_shapes=[dma((3,))],
+    )(*(pltpu.with_memory_space_constraint(r, pltpu.VMEM) for r in results)))
 
 
 def solution(mesh):

time: 102 us -> 100 us (0.980)
  Pallas kernels: 101 us -> 99.4 us
    pallas_call x1, Pallas kernels: 1.93 us -> 0.87 us  [body(): pl.pallas_call(hand_over, out_shape=tuple((out(r.shape) for r in results)...]
where the time goes in v4:
time: 100 us
  Pallas kernels  99.4 us (99%)
    pallas_call x1, Pallas kernels, body(): pl.pallas_call(functools.partial(kernel, n_sec, n_row, n_col), out_shape=...  98.5 us

profile of v4, /device:TPU:24, one launch (start us, length us, event | category | flops | bytes accessed | tf_op | source)
XLA Modules:
  0.0 100.0 jit_solution(7586130373112955245)
XLA Ops:
  0.6 98.5 %shard_map.67 = (bf16[1,192,1280]{2,1,0:T(8,128)(2,1)S(1)}, bf16[1,32,1280]{2,1,0:T(8,128)(2,1)S(1)}, bf16[1,32,2048]{2,1,0:T(8,128)(2,1)S(1)}) custom-call(bf16[1,192,1280]{2,1,0:T(8,128)(2,1)} %refs_0_.1, bf16[1,32,1280]{2,1,0:T(8,128)(2,1)} %refs_1_.1, bf16[1,32,2048]{2,1,0:T(8,128)(2,1)} %refs_2_.1, bf16[1,192,2048]{2,1,0:T(8,128)(2,1)} %refs_3_.1), custom_call_target="tpu_custom_call" | custom-call | tf_op jit(solution)/shard_map/pallas_call | solution.py:292
  99.2 0.9 shard_map.68

commit v5 on v4

--- a/solution.py
+++ b/solution.py
@@ -59,9 +59,14 @@
     for load in loads:
         load.start()
     barrier = pltpu.get_barrier_semaphore()
-    for device in [right, left, down, up] + peers:
+    for device in [right, left] + peers:
         pl.semaphore_signal(barrier, inc=1, device_id=device, device_id_type=MESH)
-    pl.semaphore_wait(barrier, 4 + len(peers))
+
+    @pl.when(sec < n_sec - 1)
+    def _():
+        pl.semaphore_signal(barrier, inc=1, device_id=up, device_id_type=MESH)
+
+    pl.semaphore_wait(barrier, 2 + len(peers) + lax.div(sec + n_sec - 1, n_sec))
     loads[0].wait()
     loads[1].wait()
 

time: 100 us -> 99.8 us (level)
  the two profiles are of different devices: /device:TPU:24 before, /device:TPU:32 now
where the time goes in v5:
time: 99.8 us; the launch traced here: 99.6 us
  Pallas kernels  99 us (99%)
    pallas_call x1, Pallas kernels, body(): pl.pallas_call(functools.partial(kernel, n_sec, n_row, n_col), out_shape=...  98.1 us

profile of v5, /device:TPU:32, one launch (start us, length us, event | category | flops | bytes accessed | tf_op | source)
XLA Modules:
  0.0 99.6 jit_solution(16334850983429196652)
XLA Ops:
  0.6 98.1 %shard_map.67 = (bf16[1,192,1280]{2,1,0:T(8,128)(2,1)S(1)}, bf16[1,32,1280]{2,1,0:T(8,128)(2,1)S(1)}, bf16[1,32,2048]{2,1,0:T(8,128)(2,1)S(1)}) custom-call(bf16[1,192,1280]{2,1,0:T(8,128)(2,1)} %refs_0_.1, bf16[1,32,1280]{2,1,0:T(8,128)(2,1)} %refs_1_.1, bf16[1,32,2048]{2,1,0:T(8,128)(2,1)} %refs_2_.1, bf16[1,192,2048]{2,1,0:T(8,128)(2,1)} %refs_3_.1), custom_call_target="tpu_custom_call" | custom-call | tf_op jit(solution)/shard_map/pallas_call | solution.py:297
  98.7 0.9 shard_map.68
